TPU v7x, 512 devices: a whole 4x4x16 slice. The times are simulated.
512 devices in a mesh: group: 8 (over z_lo), blk: 64 (over y, z_hi, x, core).
Axes of the slice: x: 4, y: 4, z: 16 (z_hi: 2, z_lo: 8; z = z_hi * 8 + z_lo), core: 2. Of those that a mesh axis runs over, the one named last changes fastest.
Arguments:
- traces: bfloat16 [2048, 3, 2, 1200], P(('group', 'blk')), may hold values from -180 to 180, as said below
- assign: int32 [2048], P(('group', 'blk')), may hold values from 0 to 3, as said below
- matching: int32 [64, 8], P('blk'), may hold values from 0 to 7, as said below
Outputs:
- between: bfloat16 [2048, 4, 3, 3, 401], P(('group', 'blk'))
- within: bfloat16 [2048, 4, 3, 3, 401], P(('group', 'blk'))
Inputs may be any that keep to these rules, and one draw needn't show every extreme that they name: traces are finite records. `assign`: each aligned block of 4 entries, one device's stations, is a permutation of 0 to 3. `matching`: each row b is one round r_b, 0 to 7, of a round-robin plan with a bye round 0: group g is paired with g XOR r_b.
All inputs are finite; a program needn't handle non-finite values.
Results may differ from a plain program's by a relative error of at most 0.0082.
Values may be sent and summed in bfloat16 or wider, within the bound.
A program may use at most 64 MiB of HBM per device.

v0:
```python
import math

import jax
import jax.numpy as jnp
from jax import lax
from jax.sharding import PartitionSpec as P

WIN = 2
NSAMP = 1200
PLEN = 1536
NF = 768
HALF = 200
LAGS = 401


EPSILON = 1e-05


def from_behind(block, axis, distance):
    devices = range(lax.axis_size(axis))
    route = [((i - distance) % len(devices), i) for i in devices]
    return lax.ppermute(block, axis, route)


def forward_table():
    sample_ids = jnp.arange(NSAMP, dtype=jnp.int32)[:, None]
    bin_ids = jnp.arange(1, NF + 1, dtype=jnp.int32)[None, :]
    phases = (sample_ids * bin_ids % PLEN).astype(jnp.float32) * (2.0 * math.pi / PLEN)
    return jnp.concatenate([jnp.cos(phases), -jnp.sin(phases)], axis=1).astype(jnp.bfloat16)


def inverse_table():
    bin_ids = jnp.arange(1, NF + 1, dtype=jnp.int32)[:, None]
    lag_ids = jnp.arange(LAGS, dtype=jnp.int32)[None, :] - HALF
    phases = (bin_ids * lag_ids % PLEN).astype(jnp.float32) * (2.0 * math.pi / PLEN)
    return jnp.concatenate([jnp.cos(phases), -jnp.sin(phases)], axis=0).astype(jnp.bfloat16)


def transform(normal, forward):
    flat_rows = normal.reshape(-1, normal.shape[-1])
    result = jnp.dot(flat_rows, forward, preferred_element_type=jnp.float32).astype(jnp.bfloat16)
    return result.reshape(normal.shape[:-1] + (forward.shape[1],))


def correlate(local_spec, remote_spec, inverse):
    half_bins = local_spec.shape[-1] // 2
    left = local_spec.astype(jnp.float32)[:, None, :, None, :, :]
    right = remote_spec.astype(jnp.float32)[None, :, None, :, :, :]
    left_re, left_im = (left[..., :half_bins], left[..., half_bins:])
    right_re, right_im = (right[..., :half_bins], right[..., half_bins:])
    real_part = jnp.sum(left_re * right_re + left_im * right_im, axis=4)
    imag_part = jnp.sum(left_re * right_im - left_im * right_re, axis=4)
    stacked = jnp.concatenate([real_part, imag_part], axis=-1).astype(jnp.bfloat16)
    lag_scale = 2.0 / (PLEN * math.sqrt(NSAMP * WIN))
    lag_values = (
        jnp.dot(stacked.reshape(-1, 2 * half_bins), inverse, preferred_element_type=jnp.float32)
        * lag_scale
    )
    return lag_values.astype(jnp.bfloat16).reshape(
        local_spec.shape[0], remote_spec.shape[0], 3, 3, inverse.shape[1]
    )


def shards(traces, assign, matching):
    station_count = traces.shape[0]
    forward = forward_table()
    inverse = inverse_table()
    slot_ids = jnp.arange(station_count, dtype=jnp.int32)
    onehot = (assign[None, :] == slot_ids[:, None]).astype(jnp.bfloat16)
    ordered = jnp.einsum("sr,rcwt->scwt", onehot, traces, preferred_element_type=jnp.float32)
    energy = jnp.mean(ordered * ordered, axis=-1, keepdims=True)
    normal = (ordered * lax.rsqrt(energy + EPSILON)).astype(jnp.bfloat16)
    spectra = transform(normal, forward)
    group_index = lax.axis_index("group")
    partner_row = matching[0]
    everything = lax.all_gather(spectra, "group", axis=0, tiled=True)
    offset = partner_row[group_index] * station_count
    remote = lax.dynamic_slice_in_dim(everything, offset, station_count, 0)
    beside = from_behind(spectra, "blk", 1)
    between = correlate(spectra, remote, inverse)
    within = correlate(spectra, beside, inverse)
    return (between, within)


def solution(mesh):
    placed = (P(("group", "blk"), None, None, None), P(("group", "blk")), P("blk", None))
    return jax.shard_map(
        shards,
        mesh=mesh,
        in_specs=placed,
        out_specs=(
            P(("group", "blk"), None, None, None, None),
            P(("group", "blk"), None, None, None, None),
        ),
        check_vma=False,
    )
```

profile of v0, /device:TPU:31, one launch (start us, length us, event | category | flops | bytes accessed | tf_op | source)
XLA Modules:
  0.0 92.5 jit_solution(3736922166715995373)
XLA Ops:
  0.6 0.0 copy-start
  0.7 0.0 copy-start.1
  0.7 16.3 %cosine_convert_fusion = (bf16[1200,768]{1,0:T(8,128)(2,1)S(1)}, bf16[1200,768]{1,0:T(8,128)(2,1)}) fusion(s32[768]{0:T(1024)S(1)} %iota_add_fusion), kind=kLoop, calls=%fused_computation.8 | loop fusion | flops 11059200 | bytes 3689472 | tf_op jit(solution)/shard_map/convert.13
  16.9 0.0 copy-done
  17.0 0.0 copy-done.1
  17.0 0.2 multiply_reduce_fusion
  17.2 0.1 multiply_convert_fusion
  17.4 0.0 copy-start.2
  17.4 2.1 %fusion.9 = bf16[24,1536]{1,0:T(8,128)(2,1)S(1)} fusion(bf16[24,1200]{1,0:T(8,128)(2,1)S(1)} %reshape.64, bf16[1200,768]{1,0:T(8,128)(2,1)} %get-tuple-element.25, bf16[1200,768]{1,0:T(8,128)(2,1)S(1)} %get-tuple-element.24), kind=kOutput, calls=%fused_computation.14 | convolution fusion | flops 95883264 | bytes 3817728 | tf_op jit(solution)/shard_map/dot_general | solution.py:41
  19.6 15.9 %collective-permute-start = (bf16[4,3,2,1536]{3,2,1,0:T(2,128)(2,1)S(1)}, bf16[4,3,2,1536]{3,2,1,0:T(2,128)(2,1)S(1)}, u32[]{:S(2)}, u32[]{:S(2)}) collective-permute-start(bf16[4,3,2,1536]{3,2,1,0:T(2,128)(2,1)S(1)} %reshape.65), channel_id=1, source_target_pairs={{63,0},{0,1},{1,2},{2,3},{3,4},{4,5},{5,6},{6,7},{7,8},{8,9},{9,10... | collective-permute-start | bytes 221192 | tf_op jit(solution)/shard_map/ppermute | solution.py:22
  35.5 41.5 %all_gather.3 = bf16[32,3,2,1536]{3,2,1,0:T(2,128)(2,1)S(1)} all-gather(bf16[4,3,2,1536]{3,2,1,0:T(2,128)(2,1)S(1)} %reshape.65), channel_id=1, replica_groups=mesh['group'=8,'blk'=64] {'group'}, dimensions={0}, use_global_device_ids=true | all-gather | bytes 663552 | tf_op jit(solution)/shard_map/all_gather | solution.py:76
  77.0 0.1 reshape.68
  77.1 0.0 copy-done.2
  77.1 0.6 fusion.33
  79.7 0.1 bitcast_convert_fusion.1
  79.8 7.1 %cosine_convert_fusion.1 = (bf16[768,401]{1,0:T(8,128)(2,1)S(1)}, bf16[768,401]{1,0:T(8,128)(2,1)S(1)}) fusion(s32[401]{0:T(512)S(1)} %iota_add_fusion.1, s32[768]{0:T(1024)S(1)} %iota_add_fusion), kind=kLoop, calls=%fused_computation.19 | loop fusion | flops 3695616 | bytes 1236548 | tf_op jit(solution)/shard_map/convert.7
  86.9 0.0 collective-permute-done
  86.9 0.1 bitcast_convert_fusion
  87.1 1.7 %add_reduce_fusion = (bf16[4,4,3,3,768]{4,1,3,2,0:T(4,128)(2,1)S(1)}, bf16[4,4,3,3,768]{4,1,3,2,0:T(4,128)(2,1)S(1)}, bf16[4,4,3,3,768]{4,1,3,2,0:T(4,128)(2,1)S(1)}, bf16[4,4,3,3,768]{4,1,3,2,0:T(4,128)(2,1)S(1)}) fusion(f32[4,3,2,768]{3,0,2,1:T(4,128)S(1)} %copy.23, f32[4,3,2,768]{3,0,2,1:T(4,128)S(1)} %copy.22, ...), kind=kLoop, calls=%fused_computation.29 | loop fusion | flops 3096576 | bytes 1327104 | tf_op jit(solution)/shard_map/reduce_sum | solution.py:51
  88.7 0.1 copy.24
  88.9 0.2 concatenate.31
  89.1 0.1 copy.25
  89.2 0.2 concatenate.32
  89.4 0.4 fusion.18
  89.8 0.1 reshape.67
  89.9 0.7 copy.27
  90.6 0.1 copy.20
  90.7 0.2 concatenate.27
  90.9 0.1 copy.21
  91.0 0.2 concatenate.28
  91.2 0.4 fusion.17
  91.7 0.1 reshape.66
  91.7 0.7 copy.26
  (13 shorter events, 0.3 us)
Async XLA Ops:
  0.6 16.3 %copy-start = (bf16[4,3,2,1200]{3,2,1,0:T(2,128)(2,1)S(1)}, bf16[4,3,2,1200]{3,2,1,0:T(2,128)(2,1)}, u32[]{:S(2)}) copy-start(bf16[4,3,2,1200]{3,2,1,0:T(2,128)(2,1)} %param.3) | copy-start | bytes 172804
  0.7 16.3 %copy-start.1 = (s32[4]{0:T(128)S(1)}, s32[4]{0:T(128)}, u32[]{:S(2)}) copy-start(s32[4]{0:T(128)} %param.4) | copy-start | bytes 52
  17.4 59.7 %copy-start.2 = (s32[1,8]{1,0:T(1,128)S(1)}, s32[1,8]{1,0:T(1,128)}, u32[]{:S(2)}) copy-start(s32[1,8]{1,0:T(1,128)} %param.5) | copy-start | bytes 100
  19.6 67.3 %collective-permute-start = (bf16[4,3,2,1536]{3,2,1,0:T(2,128)(2,1)S(1)}, bf16[4,3,2,1536]{3,2,1,0:T(2,128)(2,1)S(1)}, u32[]{:S(2)}, u32[]{:S(2)}) collective-permute-start(bf16[4,3,2,1536]{3,2,1,0:T(2,128)(2,1)S(1)} %reshape.65), channel_id=1, source_target_pairs={{63,0},{0,1},{1,2},{2,3},{3,4},{4,5},{5,6},{6,7},{7,8},{8,9},{9,10... | collective-permute-start | bytes 221192 | tf_op jit(solution)/shard_map/ppermute | solution.py:22
where the time goes:
time: 92.7 us; the launch traced here: 92.5 us
  blocking collectives  41.5 us (45%)
  other arithmetic  25.8 us (28%)
  starting transfers between devices  15.9 us (17%)
  local copies, waits for them, and re-layouts  3.24 us (3%)
  matrix products  3.16 us (3%)
  between operations  2.83 us (3%)
    all_gather x1, blocking collectives, shards(): everything = lax.all_gather(spectra, 'group', axis=0, tiled=True)  41.5 us
    another operation x2, other arithmetic  23.3 us
    ppermute x1, starting transfers between devices, from_behind(): return lax.ppermute(block, axis, route)  15.9 us
    dot_general x1, matrix products, transform(): jnp.dot(flat_rows, forward, preferred_element_type=jnp.float32)  2.1 us
  transfers between devices with their start and end apart: 1, of which 0 were waited for; matrix products, arithmetic and copies ran while one was open for 9% of the time, Pallas kernels for 0%

commit v1 on v0

v1 whole, which is shorter than its diff:
```python
import functools
import math

import jax
import jax.numpy as jnp
import ml_dtypes
import numpy as np
from jax import lax
from jax.experimental import pallas as pl
from jax.experimental.pallas import tpu as pltpu
from jax.sharding import PartitionSpec as P

WIN = 2
NSAMP = 1200
PLEN = 1536
NF = 768
HALF = 200
LAGS = 401
FAST = 256
EPSILON = 1e-05
SCALE = 2.0 / (PLEN * math.sqrt(NSAMP * WIN))
ROOT3 = math.sqrt(3) / 2
MESH = pl.DeviceIdType.MESH
bf16, f32 = jnp.bfloat16, jnp.float32

FIRSTS = ((1, 256), (2, 256), (3, 128), (6, 128))
BINS = np.concatenate([first + 6 * np.arange(count) for first, count in FIRSTS])


def tables():
    n = np.arange(FAST)
    phases = 2 * np.pi * (np.outer(n, n) % FAST) / FAST
    c, s = np.cos(phases), np.sin(phases)
    full = np.block([[c, -s], [s, c]])
    half = np.concatenate([full[:, :128], full[:, 256:384]], axis=1)
    twiddle = np.zeros((64, FAST), np.float32)
    for i, (first, _) in enumerate(FIRSTS):
        phases = 2 * np.pi * n * first / PLEN
        twiddle[16 * i : 16 * i + 8] = np.cos(phases)
        twiddle[16 * i + 8 : 16 * i + 16] = np.sin(phases)
    phases = 2 * np.pi * (np.outer(BINS, np.arange(LAGS) - HALF) % PLEN) / PLEN
    inverse = np.zeros((2 * NF, 512))
    inverse[:NF, :LAGS] = np.cos(phases)
    inverse[NF:, :LAGS] = -np.sin(phases)
    low = ml_dtypes.bfloat16
    return full.astype(low), half.astype(low), twiddle, inverse.astype(low)


def flip(index, bit):
    return index + bit - 2 * bit * lax.rem(lax.div(index, bit), 2)


def exchange_kernel(
    traces, assign, matching, quad, quad_assign, near, near_assign,
    pair, pair_assign, relay, relay_assign, sems, ready,
):
    g, b = lax.axis_index("group"), lax.axis_index("blk")
    core, x, high = lax.rem(b, 2), lax.rem(lax.div(b, 2), 4), lax.rem(lax.div(b, 8), 2)
    left, right = lax.rem(b + 63, 64), lax.rem(b + 1, 64)
    last = jnp.logical_and(x == 3, core == 1)
    first = jnp.logical_and(x == 0, core == 0)
    below = high == 0
    far = g >= 4
    up_out = jnp.logical_and(last, below)
    up_in = jnp.logical_and(first, high == 1)
    up_low = jnp.logical_and(up_out, g < 4)
    up_high = jnp.logical_and(up_out, far)
    relay_low = up_high
    relay_high = jnp.logical_and(jnp.logical_and(last, high == 1), g < 4)
    in_low = jnp.logical_and(up_in, g < 4)
    in_high = jnp.logical_and(up_in, far)
    plain_out = jnp.logical_not(up_out)
    plain_in = jnp.logical_not(up_in)

    g4, g1, g2 = flip(g, 4), flip(g, 1), flip(g, 2)
    g3 = flip(g1, 2)

    def copies(base, source, source_assign, target, target_assign, device):
        return [
            pltpu.make_async_remote_copy(
                a, t, sems.at[base + 2 * i], sems.at[base + 2 * i + 1], device_id=device, device_id_type=MESH
            )
            for i, (a, t) in enumerate(((source, target), (source_assign, target_assign)))
        ]

    def start(cs):
        for c in cs:
            c.start()

    def wait_recv(cs):
        for c in cs:
            c.wait_recv()

    def wait_send(cs):
        for c in cs:
            c.wait_send()

    barrier = pltpu.get_barrier_semaphore()

    def greet(device):
        pl.semaphore_signal(barrier, inc=1, device_id=device, device_id_type=MESH)

    for peer in (g4, g3, g2, g1):
        greet((peer, b))
    @pl.when(plain_in)
    def _():
        greet((g, left))

    @pl.when(in_low)
    def _():
        greet((g + 4, left))

    @pl.when(in_high)
    def _():
        greet((g - 4, left + 8))

    @pl.when(up_high)
    def _():
        greet((g - 4, b + 8))

    own = pltpu.make_async_copy(traces, pair.at[0], sems.at[20])
    own_assign = pltpu.make_async_copy(assign, pair_assign.at[0], sems.at[21])
    own.start()
    own_assign.start()

    count = 4 + plain_out.astype(jnp.int32) + relay_low.astype(jnp.int32) + 2 * relay_high.astype(jnp.int32)
    pl.semaphore_wait(barrier, count)

    @pl.when(relay_high)
    def _():
        pl.semaphore_signal(ready, inc=1, device_id=(lax.rem(g + 4, 8), lax.rem(b + 56, 64)), device_id_type=MESH)

    to_near = copies(0, traces, assign, near, near_assign, (g, right))

    @pl.when(plain_out)
    def _():
        start(to_near)

    to_pair = copies(4, traces, assign, pair.at[1], pair_assign.at[1], (g4, b))
    start(to_pair)
    own.wait()
    own_assign.wait()
    wait_recv(to_pair)

    pass_low = copies(0, pair.at[1], pair_assign.at[1], near, near_assign, (lax.rem(g + 4, 8), right))

    @pl.when(relay_low)
    def _():
        start(pass_low)

    round_ = matching[0, 0]
    bit = lax.rem(lax.div(round_, 4), 2)
    quad[0] = pair[bit]
    quad_assign[0] = pair_assign[bit]
    to_quad = [
        copies(4 + 4 * i, quad.at[0], quad_assign.at[0], quad.at[i], quad_assign.at[i], (peer, b))
        for i, peer in ((3, g3), (2, g2), (1, g1))
    ]
    for cs in to_quad:
        start(cs)

    to_relay = copies(22, traces, assign, relay, relay_assign, (lax.rem(g + 4, 8), lax.rem(b + 8, 64)))

    @pl.when(up_high)
    def _():
        pl.semaphore_wait(ready, 1)
        start(to_relay)

    pass_high = copies(26, relay, relay_assign, near, near_assign, (lax.rem(g + 4, 8), lax.rem(b + 57, 64)))

    @pl.when(relay_high)
    def _():
        wait_recv(to_relay)
        start(pass_high)

    for cs in to_quad:
        wait_recv(cs)

    @pl.when(jnp.logical_not(in_high))
    def _():
        wait_recv(to_near)

    @pl.when(in_high)
    def _():
        wait_recv(pass_high)

    wait_send(to_pair)
    for cs in to_quad:
        wait_send(cs)

    @pl.when(plain_out)
    def _():
        wait_send(to_near)

    @pl.when(relay_low)
    def _():
        wait_send(pass_low)

    @pl.when(up_high)
    def _():
        wait_send(to_relay)

    @pl.when(relay_high)
    def _():
        wait_send(pass_high)


def correlate_kernel(
    traces, assign, quad, quad_assign, near, near_assign, matching, full, half, twiddle, inverse,
    between, within, samples, real, imag, cross,
):
    samples[:, 1152:1280] = jnp.zeros((72, 128), f32)
    slot = lax.rem(matching[0, 0], 4)
    for r in range(4):
        mine, other, beside = assign[0, r], quad_assign[slot, r], near_assign[0, r]
        for comp in range(3):
            a = traces[r, comp].astype(f32)
            p = quad[slot, r, comp].astype(f32)
            n = near[r, comp].astype(f32)
            for w in range(2):
                samples[pl.ds(12 * w + 3 * mine + comp, 1), 0:NSAMP] = a[w : w + 1]
                samples[pl.ds(24 + 24 * w + 4 * comp + other, 1), 0:NSAMP] = p[w : w + 1]
                samples[pl.ds(36 + 24 * w + 4 * comp + beside, 1), 0:NSAMP] = n[w : w + 1]
    v = [samples[:, FAST * i : FAST * i + FAST] for i in range(5)]
    energy = v[0] * v[0]
    for i in range(1, 5):
        energy = energy + v[i] * v[i]
    scale = lax.rsqrt(jnp.sum(energy, axis=-1, keepdims=True) * (1.0 / NSAMP) + EPSILON)
    even, odd = v[0] + v[2] + v[4], v[1] + v[3]
    minus, plus = v[0] - v[3], v[0] + v[3]
    parts = (
        (minus + 0.5 * (v[1] - v[2] - v[4]), -ROOT3 * (v[1] + v[2] - v[4])),
        (plus - 0.5 * (v[1] + v[2] + v[4]), -ROOT3 * (v[1] - v[2] + v[4])),
        (even - odd, None),
        (even + odd, None),
    )
    column = 0
    for i, (re, im) in enumerate(parts):
        c = jnp.tile(twiddle[16 * i : 16 * i + 8, :], (9, 1))
        s = jnp.tile(twiddle[16 * i + 8 : 16 * i + 16, :], (9, 1))
        if im is None:
            re, im = re * c, -re * s
        else:
            re, im = re * c + im * s, im * c - re * s
        turned = jnp.concatenate([re.astype(bf16), im.astype(bf16)], axis=1)
        count = FIRSTS[i][1]
        table = full if count == FAST else half
        spectra = jnp.dot(turned, table[...], preferred_element_type=f32)
        real[:, column : column + count] = spectra[:, :count] * scale
        imag[:, column : column + count] = spectra[:, count:] * scale
        column += count
    for q in range(6):
        lanes = slice(128 * q, 128 * q + 128)
        right = [(real[24 + 24 * w : 48 + 24 * w, lanes], imag[24 + 24 * w : 48 + 24 * w, lanes]) for w in range(2)]
        for two in range(6):
            reals, imags = [], []
            for row in (2 * two, 2 * two + 1):
                re = im = None
                for w in range(2):
                    at = 12 * w + row
                    left_re = jnp.broadcast_to(real[at : at + 1, lanes], (24, 128))
                    left_im = jnp.broadcast_to(imag[at : at + 1, lanes], (24, 128))
                    right_re, right_im = right[w]
                    a = left_re * right_re + left_im * right_im
                    d = left_re * right_im - left_im * right_re
                    re, im = (a, d) if re is None else (re + a, im + d)
                reals.append(re)
                imags.append(im)
            rows = slice(48 * two, 48 * two + 48)
            cross[rows, 128 * q : 128 * q + 128] = jnp.concatenate(reals, 0).astype(bf16)
            cross[rows, NF + 128 * q : NF + 128 * q + 128] = jnp.concatenate(imags, 0).astype(bf16)
    lags = jnp.dot(cross[...], inverse[...], preferred_element_type=f32) * SCALE
    for row in range(12):
        for comp in range(3):
            at = 24 * row + 4 * comp
            between[row // 3, row % 3, comp] = lags[at : at + 4, :LAGS].astype(bf16)
            within[row // 3, row % 3, comp] = lags[at + 12 : at + 16, :LAGS].astype(bf16)


def shards(traces, assign, matching):
    vmem = pl.BlockSpec(memory_space=pltpu.VMEM)
    smem = pl.BlockSpec(memory_space=pltpu.SMEM)
    anywhere = pl.BlockSpec(memory_space=pl.ANY)
    block = traces.shape
    assign = assign.reshape(1, 4)
    quad, quad_assign, near, near_assign = pl.pallas_call(
        exchange_kernel,
        out_shape=(
            jax.ShapeDtypeStruct((4,) + block, bf16),
            jax.ShapeDtypeStruct((4, 1, 4), jnp.int32),
            jax.ShapeDtypeStruct(block, bf16),
            jax.ShapeDtypeStruct((1, 4), jnp.int32),
        ),
        in_specs=[anywhere, anywhere, smem],
        out_specs=(vmem, vmem, vmem, vmem),
        scratch_shapes=[
            pltpu.VMEM((2,) + block, bf16),
            pltpu.VMEM((2, 1, 4), jnp.int32),
            pltpu.VMEM(block, bf16),
            pltpu.VMEM((1, 4), jnp.int32),
            pltpu.SemaphoreType.DMA((30,)),
            pltpu.SemaphoreType.REGULAR,
        ],
        compiler_params=pltpu.CompilerParams(collective_id=0, has_side_effects=True),
        name="exchange",
    )(traces, assign, matching)
    full, half, twiddle, inverse = (jnp.asarray(t) for t in tables())
    between, within = pl.pallas_call(
        correlate_kernel,
        out_shape=(jax.ShapeDtypeStruct((4, 3, 3, 4, LAGS), bf16),) * 2,
        in_specs=[vmem, smem, vmem, smem, vmem, smem, smem, vmem, vmem, vmem, vmem],
        out_specs=(vmem, vmem),
        scratch_shapes=[
            pltpu.VMEM((72, 1280), f32),
            pltpu.VMEM((72, NF), f32),
            pltpu.VMEM((72, NF), f32),
            pltpu.VMEM((288, 2 * NF), bf16),
        ],
        cost_estimate=pl.CostEstimate(flops=600_000_000, bytes_accessed=3_000_000, transcendentals=0),
        name="correlate",
    )(traces, assign, quad, quad_assign.reshape(4, 4), near, near_assign, matching, full, half, twiddle, inverse)
    return tuple(jnp.transpose(v, (0, 3, 1, 2, 4)) for v in (between, within))


def solution(mesh):
    placed = (P(("group", "blk"), None, None, None), P(("group", "blk")), P("blk", None))
    return jax.shard_map(
        shards,
        mesh=mesh,
        in_specs=placed,
        out_specs=(
            P(("group", "blk"), None, None, None, None),
            P(("group", "blk"), None, None, None, None),
        ),
        check_vma=False,
    )
```

time: 92.7 us -> 33.9 us (0.37)
  the two profiles are of different devices: /device:TPU:31 before, /device:TPU:440 now
where the time goes in v1:
time: 33.9 us; the launch traced here: 33.7 us
  Pallas kernels  33 us (97%)
  between operations  0.64 us (2%)
    pallas_call x1, Pallas kernels, shards(): pl.pallas_call(exchange_kernel, out_shape=(jax.ShapeDtypeStruct((4,) + bl...  29.3 us
    pallas_call x1, Pallas kernels, shards(): pl.pallas_call(correlate_kernel, out_shape=(jax.ShapeDtypeStruct((4, 3, 3...  3.76 us

profile of v1, /device:TPU:440, one launch (start us, length us, event | category | flops | bytes accessed | tf_op | source)
XLA Modules:
  0.0 33.7 jit_solution(40009365526771198)
XLA Ops:
  0.6 29.3 %exchange.1 = (bf16[4,4,3,2,1200]{4,3,2,1,0:T(2,128)(2,1)}, s32[4,1,4]{2,1,0:T(1,128)}, bf16[4,3,2,1200]{3,2,1,0:T(2,128)(2,1)}, s32[1,4]{1,0:T(1,128)}) custom-call(bf16[4,3,2,1200]{3,2,1,0:T(2,128)(2,1)} %traces.3, s32[1,4]{1,0:T(1,128)} %bitcast.5, s32[1,8]{1,0:T(1,128)} %matching.3), custom_call_target="tpu_custom_call" | custom-call | tf_op jit(solution)/shard_map/exchange/pallas_call | solution.py:286
  29.9 3.8 %correlate.1 = (bf16[4,3,3,4,401]{4,3,2,1,0:T(4,128)(2,1)}, bf16[4,3,3,4,401]{4,3,2,1,0:T(4,128)(2,1)}) custom-call(bf16[4,3,2,1200]{3,2,1,0:T(2,128)(2,1)} %traces.3, s32[1,4]{1,0:T(1,128)} %bitcast.6, bf16[4,4,3,2,1200]{4,3,2,1,0:T(2,128)(2,1)} %get-tuple-element.8.quad, s32[4,4]{1,0:T(4,128)} %bitcast.4, bf16[4,3,2,1200]{3,2,1,0:T(2,128)(2,1)} %get-tuple-element.10.near, ...), custom_call_target="tpu_custom_call" | custom-call | flops 600000000 | bytes 3000000 | tf_op jit(solution)/shard_map/correlate/pallas_call | solution.py:308

commit v2 on v1

--- a/solution.py
+++ b/solution.py
@@ -52,25 +52,21 @@
 
 def exchange_kernel(
     traces, assign, matching, quad, quad_assign, near, near_assign,
-    pair, pair_assign, relay, relay_assign, sems, ready,
+    pair, pair_assign, sems, ready,
 ):
     g, b = lax.axis_index("group"), lax.axis_index("blk")
     core, x, high = lax.rem(b, 2), lax.rem(lax.div(b, 2), 4), lax.rem(lax.div(b, 8), 2)
     left, right = lax.rem(b + 63, 64), lax.rem(b + 1, 64)
     last = jnp.logical_and(x == 3, core == 1)
     first = jnp.logical_and(x == 0, core == 0)
-    below = high == 0
-    far = g >= 4
+    below, above = high == 0, high == 1
     up_out = jnp.logical_and(last, below)
-    up_in = jnp.logical_and(first, high == 1)
-    up_low = jnp.logical_and(up_out, g < 4)
-    up_high = jnp.logical_and(up_out, far)
-    relay_low = up_high
-    relay_high = jnp.logical_and(jnp.logical_and(last, high == 1), g < 4)
-    in_low = jnp.logical_and(up_in, g < 4)
-    in_high = jnp.logical_and(up_in, far)
+    up_in = jnp.logical_and(first, above)
+    near_half = g < 4
+    far_half = g >= 4
     plain_out = jnp.logical_not(up_out)
     plain_in = jnp.logical_not(up_in)
+    opposite = lax.rem(g + 4, 8)
 
     g4, g1, g2 = flip(g, 4), flip(g, 1), flip(g, 2)
     g3 = flip(g1, 2)
@@ -97,38 +93,47 @@
 
     barrier = pltpu.get_barrier_semaphore()
 
+    def one(flag):
+        return flag.astype(jnp.int32)
+
     def greet(device):
         pl.semaphore_signal(barrier, inc=1, device_id=device, device_id_type=MESH)
 
-    for peer in (g4, g3, g2, g1):
-        greet((peer, b))
+    def tell(i, device):
+        pl.semaphore_signal(ready.at[i], inc=1, device_id=device, device_id_type=MESH)
+
+    peers = (g4, g1, g2, g3)
+    ordered = jnp.logical_or(below, last)
+    mutual = jnp.logical_not(ordered)
+    witness = jnp.logical_and(up_in, near_half)
+    count = one(plain_out) + 2 * one(witness)
+    for peer in peers:
+        count = count + one(jnp.logical_or(mutual, peer < g))
+
+        @pl.when(jnp.logical_or(mutual, peer > g))
+        def _():
+            greet((peer, b))
+
     @pl.when(plain_in)
     def _():
         greet((g, left))
 
-    @pl.when(in_low)
-    def _():
-        greet((g + 4, left))
-
-    @pl.when(in_high)
-    def _():
-        greet((g - 4, left + 8))
-
-    @pl.when(up_high)
-    def _():
-        greet((g - 4, b + 8))
+    @pl.when(jnp.logical_and(up_out, near_half))
+    def _():
+        greet((g, right))
+
+    @pl.when(jnp.logical_and(up_out, far_half))
+    def _():
+        greet((opposite, right))
 
     own = pltpu.make_async_copy(traces, pair.at[0], sems.at[20])
     own_assign = pltpu.make_async_copy(assign, pair_assign.at[0], sems.at[21])
     own.start()
     own_assign.start()
 
-    count = 4 + plain_out.astype(jnp.int32) + relay_low.astype(jnp.int32) + 2 * relay_high.astype(jnp.int32)
-    pl.semaphore_wait(barrier, count)
-
-    @pl.when(relay_high)
-    def _():
-        pl.semaphore_signal(ready, inc=1, device_id=(lax.rem(g + 4, 8), lax.rem(b + 56, 64)), device_id_type=MESH)
+    @pl.when(count > 0)
+    def _():
+        pl.semaphore_wait(barrier, count)
 
     to_near = copies(0, traces, assign, near, near_assign, (g, right))
 
@@ -136,73 +141,54 @@
     def _():
         start(to_near)
 
+    for i, peer in enumerate(peers):
+
+        @pl.when(jnp.logical_and(ordered, peer < g))
+        def _():
+            tell(i, (peer, b))
+
+    @pl.when(witness)
+    def _():
+        tell(4, (g, left))
+        tell(4, (opposite, left))
+
+    def wait_ready(i):
+        @pl.when(jnp.logical_and(ordered, peers[i] > g))
+        def _():
+            pl.semaphore_wait(ready.at[i], 1)
+
     to_pair = copies(4, traces, assign, pair.at[1], pair_assign.at[1], (g4, b))
+    wait_ready(0)
     start(to_pair)
+
+    def step_up():
+        pl.semaphore_wait(ready.at[4], 1)
+        start(to_near)
+
+    pl.when(jnp.logical_and(up_out, far_half))(step_up)
     own.wait()
     own_assign.wait()
     wait_recv(to_pair)
-
-    pass_low = copies(0, pair.at[1], pair_assign.at[1], near, near_assign, (lax.rem(g + 4, 8), right))
-
-    @pl.when(relay_low)
-    def _():
-        start(pass_low)
 
     round_ = matching[0, 0]
     bit = lax.rem(lax.div(round_, 4), 2)
     quad[0] = pair[bit]
     quad_assign[0] = pair_assign[bit]
-    to_quad = [
-        copies(4 + 4 * i, quad.at[0], quad_assign.at[0], quad.at[i], quad_assign.at[i], (peer, b))
-        for i, peer in ((3, g3), (2, g2), (1, g1))
-    ]
-    for cs in to_quad:
-        start(cs)
-
-    to_relay = copies(22, traces, assign, relay, relay_assign, (lax.rem(g + 4, 8), lax.rem(b + 8, 64)))
-
-    @pl.when(up_high)
-    def _():
-        pl.semaphore_wait(ready, 1)
-        start(to_relay)
-
-    pass_high = copies(26, relay, relay_assign, near, near_assign, (lax.rem(g + 4, 8), lax.rem(b + 57, 64)))
-
-    @pl.when(relay_high)
-    def _():
-        wait_recv(to_relay)
-        start(pass_high)
+    to_quad = []
+    for i in (2, 3, 1):
+        to_quad.append(copies(4 + 4 * i, quad.at[0], quad_assign.at[0], quad.at[i], quad_assign.at[i], (peers[i], b)))
+        wait_ready(i)
+        start(to_quad[-1])
+
+    pl.when(jnp.logical_and(up_out, near_half))(step_up)
 
     for cs in to_quad:
         wait_recv(cs)
-
-    @pl.when(jnp.logical_not(in_high))
-    def _():
-        wait_recv(to_near)
-
-    @pl.when(in_high)
-    def _():
-        wait_recv(pass_high)
-
+    wait_recv(to_near)
     wait_send(to_pair)
     for cs in to_quad:
         wait_send(cs)
-
-    @pl.when(plain_out)
-    def _():
-        wait_send(to_near)
-
-    @pl.when(relay_low)
-    def _():
-        wait_send(pass_low)
-
-    @pl.when(up_high)
-    def _():
-        wait_send(to_relay)
-
-    @pl.when(relay_high)
-    def _():
-        wait_send(pass_high)
+    wait_send(to_near)
 
 
 def correlate_kernel(
@@ -296,10 +282,8 @@
         scratch_shapes=[
             pltpu.VMEM((2,) + block, bf16),
             pltpu.VMEM((2, 1, 4), jnp.int32),
-            pltpu.VMEM(block, bf16),
-            pltpu.VMEM((1, 4), jnp.int32),
-            pltpu.SemaphoreType.DMA((30,)),
-            pltpu.SemaphoreType.REGULAR,
+            pltpu.SemaphoreType.DMA((22,)),
+            pltpu.SemaphoreType.REGULAR((5,)),
         ],
         compiler_params=pltpu.CompilerParams(collective_id=0, has_side_effects=True),
         name="exchange",

time: 33.9 us -> 28.7 us (0.85)
  the two profiles are of different devices: /device:TPU:440 before, /device:TPU:128 now
where the time goes in v2:
time: 28.7 us; the launch traced here: 28.4 us
  Pallas kernels  27.8 us (97%)
  between operations  0.64 us (2%)
    pallas_call x1, Pallas kernels, shards(): pl.pallas_call(exchange_kernel, out_shape=(jax.ShapeDtypeStruct((4,) + bl...  24 us
    pallas_call x1, Pallas kernels, shards(): pl.pallas_call(correlate_kernel, out_shape=(jax.ShapeDtypeStruct((4, 3, 3...  3.76 us

profile of v2, /device:TPU:128, one launch (start us, length us, event | category | flops | bytes accessed | tf_op | source)
XLA Modules:
  0.0 28.4 jit_solution(6820839025479460348)
XLA Ops:
  0.6 24.0 %exchange.1 = (bf16[4,4,3,2,1200]{4,3,2,1,0:T(2,128)(2,1)}, s32[4,1,4]{2,1,0:T(1,128)}, bf16[4,3,2,1200]{3,2,1,0:T(2,128)(2,1)}, s32[1,4]{1,0:T(1,128)}) custom-call(bf16[4,3,2,1200]{3,2,1,0:T(2,128)(2,1)} %traces.3, s32[1,4]{1,0:T(1,128)} %bitcast.5, s32[1,8]{1,0:T(1,128)} %matching.3), custom_call_target="tpu_custom_call" | custom-call | tf_op jit(solution)/shard_map/exchange/pallas_call | solution.py:272
  24.7 3.8 %correlate.1 = (bf16[4,3,3,4,401]{4,3,2,1,0:T(4,128)(2,1)}, bf16[4,3,3,4,401]{4,3,2,1,0:T(4,128)(2,1)}) custom-call(bf16[4,3,2,1200]{3,2,1,0:T(2,128)(2,1)} %traces.3, s32[1,4]{1,0:T(1,128)} %bitcast.6, bf16[4,4,3,2,1200]{4,3,2,1,0:T(2,128)(2,1)} %get-tuple-element.8.quad, s32[4,4]{1,0:T(4,128)} %bitcast.4, bf16[4,3,2,1200]{3,2,1,0:T(2,128)(2,1)} %get-tuple-element.10.near, ...), custom_call_target="tpu_custom_call" | custom-call | flops 600000000 | bytes 3000000 | tf_op jit(solution)/shard_map/correlate/pallas_call | solution.py:292

commit v3 on v2

v3 whole, which is shorter than its diff:
```python
import functools
import math

import jax
import jax.numpy as jnp
import ml_dtypes
import numpy as np
from jax import lax
from jax.experimental import pallas as pl
from jax.experimental.pallas import tpu as pltpu
from jax.sharding import PartitionSpec as P

WIN = 2
NSAMP = 1200
PLEN = 1536
NF = 768
HALF = 200
LAGS = 401
FAST = 256
EPSILON = 1e-05
SCALE = 2.0 / (PLEN * math.sqrt(NSAMP * WIN))
ROOT3 = math.sqrt(3) / 2
MESH = pl.DeviceIdType.MESH
bf16, f32 = jnp.bfloat16, jnp.float32

FIRSTS = ((1, 256), (2, 256), (3, 128), (6, 128))
BINS = np.concatenate([first + 6 * np.arange(count) for first, count in FIRSTS])


def tables():
    n = np.arange(FAST)
    phases = 2 * np.pi * (np.outer(n, n) % FAST) / FAST
    c, s = np.cos(phases), np.sin(phases)
    full = np.block([[c, -s], [s, c]])
    half = np.concatenate([full[:, :128], full[:, 256:384]], axis=1)
    twiddle = np.zeros((64, FAST), np.float32)
    for i, (first, _) in enumerate(FIRSTS):
        phases = 2 * np.pi * n * first / PLEN
        twiddle[16 * i : 16 * i + 8] = np.cos(phases)
        twiddle[16 * i + 8 : 16 * i + 16] = np.sin(phases)
    phases = 2 * np.pi * (np.outer(BINS, np.arange(LAGS) - HALF) % PLEN) / PLEN
    inverse = np.zeros((2 * NF, 512))
    inverse[:NF, :LAGS] = np.cos(phases)
    inverse[NF:, :LAGS] = -np.sin(phases)
    low = ml_dtypes.bfloat16
    return full.astype(low), half.astype(low), twiddle, inverse.astype(low)


def flip(index, bit):
    return index + bit - 2 * bit * lax.rem(lax.div(index, bit), 2)


def inverse_order(assign):
    rows = [assign(r) for r in range(4)]
    order = []
    for s in range(4):
        found = 0
        for r in range(1, 4):
            found = jnp.where(rows[r] == s, r, found)
        order.append(found)
    return order


def load_samples(samples, block, order, row):
    for station in range(4):
        for comp in range(3):
            both = block(order[station], comp).astype(f32)
            for w in range(2):
                at = 16 * w + row(station, comp)
                samples[at : at + 1, 0:NSAMP] = both[w : w + 1]


def transform(samples, full, half, twiddle, real, imag):
    v = [samples[:, FAST * i : FAST * i + FAST] for i in range(5)]
    energy = v[0] * v[0]
    for i in range(1, 5):
        energy = energy + v[i] * v[i]
    scale = lax.rsqrt(jnp.sum(energy, axis=-1, keepdims=True) * (1.0 / NSAMP) + EPSILON)
    even, odd = v[0] + v[2] + v[4], v[1] + v[3]
    minus, plus = v[0] - v[3], v[0] + v[3]
    parts = (
        (minus + 0.5 * (v[1] - v[2] - v[4]), -ROOT3 * (v[1] + v[2] - v[4])),
        (plus - 0.5 * (v[1] + v[2] + v[4]), -ROOT3 * (v[1] - v[2] + v[4])),
        (even - odd, None),
        (even + odd, None),
    )
    turned = []
    for i, (re, im) in enumerate(parts):
        c = jnp.tile(twiddle[16 * i : 16 * i + 8, :], (4, 1))
        s = jnp.tile(twiddle[16 * i + 8 : 16 * i + 16, :], (4, 1))
        if im is None:
            re, im = re * c, -re * s
        else:
            re, im = re * c + im * s, im * c - re * s
        turned.append(jnp.concatenate([re.astype(bf16), im.astype(bf16)], axis=1))
    column = 0
    for i, table, count in ((0, full, FAST), (2, half, 128)):
        both = jnp.concatenate(turned[i : i + 2], axis=0)
        spectra = jnp.dot(both, table[...], preferred_element_type=f32)
        for k in range(2):
            real[:, column : column + count] = spectra[32 * k : 32 * k + 32, :count] * scale
            imag[:, column : column + count] = spectra[32 * k : 32 * k + 32, count:] * scale
            column += count


def multiply(left, right, cross):
    for q in range(3):
        lanes = slice(256 * q, 256 * q + 256)
        other = [[part[16 * w : 16 * w + 16, lanes] for part in right] for w in range(2)]
        for row in range(12):
            re = im = None
            for w in range(2):
                at = 16 * w + row
                left_re = jnp.broadcast_to(left[0][at : at + 1, lanes], (16, 256))
                left_im = jnp.broadcast_to(left[1][at : at + 1, lanes], (16, 256))
                right_re, right_im = other[w]
                a = left_re * right_re + left_im * right_im
                d = left_re * right_im - left_im * right_re
                re, im = (a, d) if re is None else (re + a, im + d)
            cross[16 * row : 16 * row + 16, lanes] = re.astype(bf16)
            cross[16 * row : 16 * row + 16, NF + 256 * q : NF + 256 * q + 256] = im.astype(bf16)


def correlate_kernel(
    traces, assign, matching_hbm, full_hbm, half_hbm, twiddle_hbm, inverse_hbm,
    between, within,
    own, pair, quad, near, matching, own_assign, pair_assign, quad_assign, near_assign,
    full, half, twiddle, inverse, samples, left_re, left_im, right_re, right_im, cross, lags,
    sems, local, ready,
):
    g, b = lax.axis_index("group"), lax.axis_index("blk")
    core, x, high = lax.rem(b, 2), lax.rem(lax.div(b, 2), 4), lax.rem(lax.div(b, 8), 2)
    left, right = lax.rem(b + 63, 64), lax.rem(b + 1, 64)
    last = jnp.logical_and(x == 3, core == 1)
    first = jnp.logical_and(x == 0, core == 0)
    below, above = high == 0, high == 1
    up_out = jnp.logical_and(last, below)
    up_in = jnp.logical_and(first, above)
    near_half = g < 4
    far_half = g >= 4
    plain_out = jnp.logical_not(up_out)
    plain_in = jnp.logical_not(up_in)
    opposite = lax.rem(g + 4, 8)

    g4, g1, g2 = flip(g, 4), flip(g, 1), flip(g, 2)
    g3 = flip(g1, 2)

    def copies(base, source, source_assign, target, target_assign, device):
        return [
            pltpu.make_async_remote_copy(
                a, t, sems.at[base + 2 * i], sems.at[base + 2 * i + 1], device_id=device, device_id_type=MESH
            )
            for i, (a, t) in enumerate(((source, target), (source_assign, target_assign)))
        ]

    def start(cs):
        for c in cs:
            c.start()

    def wait_recv(cs):
        for c in cs:
            c.wait_recv()

    def wait_send(cs):
        for c in cs:
            c.wait_send()

    barrier = pltpu.get_barrier_semaphore()

    def one(flag):
        return flag.astype(jnp.int32)

    def greet(device):
        pl.semaphore_signal(barrier, inc=1, device_id=device, device_id_type=MESH)

    def tell(i, device):
        pl.semaphore_signal(ready.at[i], inc=1, device_id=device, device_id_type=MESH)

    peers = (g4, g1, g2, g3)
    ordered = jnp.logical_or(below, last)
    mutual = jnp.logical_not(ordered)
    witness = jnp.logical_and(up_in, near_half)
    count = one(plain_out) + 2 * one(witness)
    for peer in peers:
        count = count + one(jnp.logical_or(mutual, peer < g))

        @pl.when(jnp.logical_or(mutual, peer > g))
        def _():
            greet((peer, b))

    @pl.when(plain_in)
    def _():
        greet((g, left))

    @pl.when(jnp.logical_and(up_out, near_half))
    def _():
        greet((g, right))

    @pl.when(jnp.logical_and(up_out, far_half))
    def _():
        greet((opposite, right))

    arrivals = [
        pltpu.make_async_copy(source, target, local.at[i])
        for i, (source, target) in enumerate(
            (
                (traces, own),
                (traces, pair.at[0]),
                (assign, pair_assign.at[0]),
                (assign, own_assign),
                (matching_hbm, matching),
                (full_hbm, full),
                (half_hbm, half),
                (twiddle_hbm, twiddle),
                (inverse_hbm, inverse),
            )
        )
    ]
    for c in arrivals:
        c.start()

    @pl.when(count > 0)
    def _():
        pl.semaphore_wait(barrier, count)

    to_near = copies(0, traces, assign, near, near_assign, (g, right))

    @pl.when(plain_out)
    def _():
        start(to_near)

    for i, peer in enumerate(peers):

        @pl.when(jnp.logical_and(ordered, peer < g))
        def _():
            tell(i, (peer, b))

    @pl.when(witness)
    def _():
        tell(4, (g, left))
        tell(4, (opposite, left))

    def wait_ready(i):
        @pl.when(jnp.logical_and(ordered, peers[i] > g))
        def _():
            pl.semaphore_wait(ready.at[i], 1)

    to_pair = copies(4, traces, assign, pair.at[1], pair_assign.at[1], (g4, b))
    wait_ready(0)
    start(to_pair)

    def step_up():
        pl.semaphore_wait(ready.at[4], 1)
        start(to_near)

    pl.when(jnp.logical_and(up_out, far_half))(step_up)
    samples[...] = jnp.zeros(samples.shape, f32)
    for c in arrivals:
        c.wait()
    order = inverse_order(lambda r: own_assign[0, r])
    load_samples(samples, lambda r, comp: own[r, comp], order, lambda station, comp: 3 * station + comp)
    transform(samples, full, half, twiddle, left_re, left_im)
    wait_recv(to_pair)

    round_ = matching[0, 0]
    bit = lax.rem(lax.div(round_, 4), 2)
    quad[0] = pair[bit]
    for r in range(4):
        quad_assign[0, 0, r] = pair_assign[bit, 0, r]
    to_quad = []
    for i in (2, 3, 1):
        to_quad.append(copies(4 + 4 * i, quad.at[0], quad_assign.at[0], quad.at[i], quad_assign.at[i], (peers[i], b)))
        wait_ready(i)
        start(to_quad[-1])

    pl.when(jnp.logical_and(up_out, near_half))(step_up)

    samples[...] = jnp.zeros(samples.shape, f32)
    slot = lax.rem(round_, 4)
    results = [pltpu.make_async_copy(lags.at[k], out, local.at[9 + k]) for k, out in enumerate((within, between))]

    def other_row(station, comp):
        return 4 * comp + station

    def side(step, carry):
        which = step + one(first) - 2 * step * one(first)

        @pl.when(which == 0)
        def _():
            wait_recv(to_near)
            order = inverse_order(lambda r: near_assign[0, r])
            load_samples(samples, lambda r, comp: near[r, comp], order, other_row)

        @pl.when(which == 1)
        def _():
            for cs in to_quad:
                wait_recv(cs)
            order = inverse_order(lambda r: quad_assign[slot, 0, r])
            load_samples(samples, lambda r, comp: quad[slot, r, comp], order, other_row)

        transform(samples, full, half, twiddle, right_re, right_im)
        multiply((left_re, left_im), (right_re, right_im), cross)
        result = jnp.dot(cross[...], inverse[...], preferred_element_type=f32) * SCALE
        for row in range(12):
            for comp in range(3):
                at = 16 * row + 4 * comp
                lags[which, row // 3, row % 3, comp] = result[at : at + 4, :LAGS].astype(bf16)
        for k in range(2):
            pl.when(which == k)(results[k].start)
        return carry

    lax.fori_loop(0, 2, side, 0)
    wait_send(to_pair)
    for cs in to_quad:
        wait_send(cs)
    wait_send(to_near)
    for c in results:
        c.wait()


def shards(traces, assign, matching):
    anywhere = pl.BlockSpec(memory_space=pl.ANY)
    hbm = pl.BlockSpec(memory_space=pltpu.HBM)
    block = traces.shape
    assign = assign.reshape(1, 4)
    tables_ = [jnp.asarray(t) for t in tables()]
    result = (4, 3, 3, 4, LAGS)
    between, within = pl.pallas_call(
        correlate_kernel,
        out_shape=(jax.ShapeDtypeStruct(result, bf16),) * 2,
        in_specs=[hbm] * 7,
        out_specs=(anywhere, anywhere),
        scratch_shapes=[
            pltpu.VMEM(block, bf16),
            pltpu.VMEM((2,) + block, bf16),
            pltpu.VMEM((4,) + block, bf16),
            pltpu.VMEM(block, bf16),
            pltpu.SMEM(matching.shape, jnp.int32),
            pltpu.SMEM((1, 4), jnp.int32),
            pltpu.SMEM((2, 1, 4), jnp.int32),
            pltpu.SMEM((4, 1, 4), jnp.int32),
            pltpu.SMEM((1, 4), jnp.int32),
            *(pltpu.VMEM(t.shape, t.dtype) for t in tables_),
            pltpu.VMEM((32, 1280), f32),
            *(pltpu.VMEM((32, NF), f32) for _ in range(4)),
            pltpu.VMEM((192, 2 * NF), bf16),
            pltpu.VMEM((2,) + result, bf16),
            pltpu.SemaphoreType.DMA((20,)),
            pltpu.SemaphoreType.DMA((11,)),
            pltpu.SemaphoreType.REGULAR((5,)),
        ],
        compiler_params=pltpu.CompilerParams(collective_id=0, has_side_effects=True, vmem_limit_bytes=32 << 20),
        name="correlate",
    )(*(pltpu.with_memory_space_constraint(v, pltpu.HBM) for v in (traces, assign, matching, *tables_)))
    return tuple(jnp.transpose(v, (0, 3, 1, 2, 4)) for v in (between, within))


def solution(mesh):
    placed = (P(("group", "blk"), None, None, None), P(("group", "blk")), P("blk", None))
    return jax.shard_map(
        shards,
        mesh=mesh,
        in_specs=placed,
        out_specs=(
            P(("group", "blk"), None, None, None, None),
            P(("group", "blk"), None, None, None, None),
        ),
        check_vma=False,
    )
```

time: 28.7 us -> 26.8 us (0.934)
  Pallas kernels: 27.8 us -> 24.7 us
  local copies, waits for them, and re-layouts: 0 us -> 1.32 us
    pallas_call x2 -> x1, Pallas kernels: 27.8 us -> 24.7 us  [shards(): pl.pallas_call(correlate_kernel, out_shape=(jax.ShapeDtypeStruct(result,...]
    unnamed x0 -> x2, local copies, waits for them, and re-layouts: none -> 1.32 us
where the time goes in v3:
time: 26.8 us; the launch traced here: 26.6 us
  Pallas kernels  24.7 us (92%)
  local copies, waits for them, and re-layouts  1.32 us (5%)
  between operations  0.64 us (2%)
    pallas_call x1, Pallas kernels, shards(): pl.pallas_call(correlate_kernel, out_shape=(jax.ShapeDtypeStruct(result,...  24.7 us
    unnamed x2, local copies, waits for them, and re-layouts  1.32 us

profile of v3, /device:TPU:128, one launch (start us, length us, event | category | flops | bytes accessed | tf_op | source)
XLA Modules:
  0.0 26.6 jit_solution(9097569985639047789)
XLA Ops:
  0.6 24.7 %correlate.1 = (bf16[4,3,3,4,401]{4,3,2,1,0:T(4,128)(2,1)S(1)}, bf16[4,3,3,4,401]{4,3,2,1,0:T(4,128)(2,1)S(1)}) custom-call(bf16[4,3,2,1200]{3,2,1,0:T(2,128)(2,1)} %traces.1, s32[1,4]{1,0:T(1,128)} %bitcast.5, s32[1,8]{1,0:T(1,128)} %matching_hbm.1, bf16[512,512]{1,0:T(8,128)(2,1)} %constant.8.clone.full_hbm, bf16[512,256]{1,0:T(8,128)(2,1)} %constant.9.clone.half_hbm, ...), custom_call_target="tpu_custom_call" | custom-call | tf_op jit(solution)/shard_map/correlate/pallas_call | solution.py:328
  25.3 0.7 %copy.11 = bf16[4,4,3,3,401]{4,1,3,2,0:T(4,128)(2,1)} copy(bf16[4,4,3,3,401]{4,1,3,2,0:T(4,128)(2,1)S(1)} %bitcast.4) | data formatting | bytes 230976
  26.0 0.7 %copy.12 = bf16[4,4,3,3,401]{4,1,3,2,0:T(4,128)(2,1)} copy(bf16[4,4,3,3,401]{4,1,3,2,0:T(4,128)(2,1)S(1)} %bitcast.3) | data formatting | bytes 230976

commit v4 on v3

--- a/solution.py
+++ b/solution.py
@@ -121,9 +121,15 @@
             cross[16 * row : 16 * row + 16, NF + 256 * q : NF + 256 * q + 256] = im.astype(bf16)
 
 
+def exclusive_or(a, b):
+    a1, b1 = lax.div(a, 2), lax.div(b, 2)
+    a0, b0 = a - 2 * a1, b - 2 * b1
+    return 2 * (a1 + b1 - 2 * a1 * b1) + a0 + b0 - 2 * a0 * b0
+
+
 def correlate_kernel(
     traces, assign, matching_hbm, full_hbm, half_hbm, twiddle_hbm, inverse_hbm,
-    between, within,
+    out,
     own, pair, quad, near, matching, own_assign, pair_assign, quad_assign, near_assign,
     full, half, twiddle, inverse, samples, left_re, left_im, right_re, right_im, cross, lags,
     sems, local, ready,
@@ -267,17 +273,36 @@
     quad[0] = pair[bit]
     for r in range(4):
         quad_assign[0, 0, r] = pair_assign[bit, 0, r]
+    place = lax.rem(g, 4)
     to_quad = []
-    for i in (2, 3, 1):
-        to_quad.append(copies(4 + 4 * i, quad.at[0], quad_assign.at[0], quad.at[i], quad_assign.at[i], (peers[i], b)))
-        wait_ready(i)
-        start(to_quad[-1])
+    for k in range(3):
+        target = k + one(place <= k)
+        i = exclusive_or(place, target)
+        peer = g - place + target
+        cs = copies(4 + 4 * i, quad.at[0], quad_assign.at[0], quad.at[i], quad_assign.at[i], (peer, b))
+
+        @pl.when(jnp.logical_and(ordered, peer > g))
+        def _():
+            pl.semaphore_wait(ready.at[i], 1)
+
+        start(cs)
+        to_quad.append(cs)
+        if k == 0:
+
+            @pl.when(below)
+            def _():
+                wait_send(cs)
+
+    from_quad = [
+        copies(4 + 4 * i, quad.at[0], quad_assign.at[0], quad.at[i], quad_assign.at[i], (peers[i], b))
+        for i in range(1, 4)
+    ]
 
     pl.when(jnp.logical_and(up_out, near_half))(step_up)
 
     samples[...] = jnp.zeros(samples.shape, f32)
     slot = lax.rem(round_, 4)
-    results = [pltpu.make_async_copy(lags.at[k], out, local.at[9 + k]) for k, out in enumerate((within, between))]
+    results = [pltpu.make_async_copy(lags.at[k], out.at[k], local.at[9 + k]) for k in range(2)]
 
     def other_row(station, comp):
         return 4 * comp + station
@@ -293,7 +318,7 @@
 
         @pl.when(which == 1)
         def _():
-            for cs in to_quad:
+            for cs in from_quad:
                 wait_recv(cs)
             order = inverse_order(lambda r: quad_assign[slot, 0, r])
             load_samples(samples, lambda r, comp: quad[slot, r, comp], order, other_row)
@@ -311,7 +336,8 @@
 
     lax.fori_loop(0, 2, side, 0)
     wait_send(to_pair)
-    for cs in to_quad:
+    pl.when(above)(lambda: wait_send(to_quad[0]))
+    for cs in to_quad[1:]:
         wait_send(cs)
     wait_send(to_near)
     for c in results:
@@ -324,12 +350,12 @@
     block = traces.shape
     assign = assign.reshape(1, 4)
     tables_ = [jnp.asarray(t) for t in tables()]
-    result = (4, 3, 3, 4, LAGS)
-    between, within = pl.pallas_call(
+    result = (2, 4, 3, 3, 4, LAGS)
+    both = pl.pallas_call(
         correlate_kernel,
-        out_shape=(jax.ShapeDtypeStruct(result, bf16),) * 2,
+        out_shape=jax.ShapeDtypeStruct(result, bf16),
         in_specs=[hbm] * 7,
-        out_specs=(anywhere, anywhere),
+        out_specs=anywhere,
         scratch_shapes=[
             pltpu.VMEM(block, bf16),
             pltpu.VMEM((2,) + block, bf16),
@@ -344,7 +370,7 @@
             pltpu.VMEM((32, 1280), f32),
             *(pltpu.VMEM((32, NF), f32) for _ in range(4)),
             pltpu.VMEM((192, 2 * NF), bf16),
-            pltpu.VMEM((2,) + result, bf16),
+            pltpu.VMEM(result, bf16),
             pltpu.SemaphoreType.DMA((20,)),
             pltpu.SemaphoreType.DMA((11,)),
             pltpu.SemaphoreType.REGULAR((5,)),
@@ -352,7 +378,7 @@
         compiler_params=pltpu.CompilerParams(collective_id=0, has_side_effects=True, vmem_limit_bytes=32 << 20),
         name="correlate",
     )(*(pltpu.with_memory_space_constraint(v, pltpu.HBM) for v in (traces, assign, matching, *tables_)))
-    return tuple(jnp.transpose(v, (0, 3, 1, 2, 4)) for v in (between, within))
+    return tuple(jnp.transpose(v, (0, 3, 1, 2, 4)) for v in (both[1], both[0]))
 
 
 def solution(mesh):

time: 26.8 us -> 25.1 us (0.937)
  the two profiles are of different devices: /device:TPU:128 before, /device:TPU:160 now
where the time goes in v4:
time: 25.1 us; the launch traced here: 25 us
  Pallas kernels  23.5 us (94%)
  local copies, waits for them, and re-layouts  0.81 us (3%)
  between operations  0.64 us (3%)
    pallas_call x1, Pallas kernels, shards(): pl.pallas_call(correlate_kernel, out_shape=jax.ShapeDtypeStruct(result, b...  23.5 us
    transpose x1, local copies, waits for them, and re-layouts, shards(): jnp.transpose(v, (0, 3, 1, 2, 4))  0.81 us

profile of v4, /device:TPU:160, one launch (start us, length us, event | category | flops | bytes accessed | tf_op | source)
XLA Modules:
  0.0 25.0 jit_solution(6245813671707546648)
XLA Ops:
  0.6 23.5 %correlate.1 = bf16[2,4,3,3,4,401]{5,4,3,2,1,0:T(4,128)(2,1)S(1)} custom-call(bf16[4,3,2,1200]{3,2,1,0:T(2,128)(2,1)} %traces.1, s32[1,4]{1,0:T(1,128)} %bitcast.9, s32[1,8]{1,0:T(1,128)} %matching_hbm.1, bf16[512,512]{1,0:T(8,128)(2,1)} %constant.8.clone.full_hbm, bf16[512,256]{1,0:T(8,128)(2,1)} %constant.9.clone.half_hbm, ...), custom_call_target="tpu_custom_call" | custom-call | tf_op jit(solution)/shard_map/correlate/pallas_call | solution.py:354
  24.2 0.8 %slice_bitcast_fusion = (bf16[4,4,3,3,401]{4,1,3,2,0:T(4,128)(2,1)}, bf16[4,4,3,3,401]{4,1,3,2,0:T(4,128)(2,1)}) fusion(bf16[2,4,3,3,4,401]{5,4,3,2,1,0:T(4,128)(2,1)S(1)} %correlate.1), kind=kLoop, calls=%fused_computation | loop fusion | bytes 461952 | tf_op jit(solution)/shard_map/transpose | solution.py:381

commit v5 on v4

--- a/solution.py
+++ b/solution.py
@@ -131,7 +131,7 @@
     traces, assign, matching_hbm, full_hbm, half_hbm, twiddle_hbm, inverse_hbm,
     out,
     own, pair, quad, near, matching, own_assign, pair_assign, quad_assign, near_assign,
-    full, half, twiddle, inverse, samples, left_re, left_im, right_re, right_im, cross, lags,
+    full, half, twiddle, inverse, samples, left_re, left_im, right_re, right_im, cross,
     sems, local, ready,
 ):
     g, b = lax.axis_index("group"), lax.axis_index("blk")
@@ -187,12 +187,20 @@
     mutual = jnp.logical_not(ordered)
     witness = jnp.logical_and(up_in, near_half)
     count = one(plain_out) + 2 * one(witness)
+    source = jnp.logical_and(jnp.logical_and(above, last), near_half)
+    count = count + 3 * one(jnp.logical_and(jnp.logical_and(above, last), far_half))
+    settled = jnp.logical_not(source)
     for peer in peers:
-        count = count + one(jnp.logical_or(mutual, peer < g))
-
-        @pl.when(jnp.logical_or(mutual, peer > g))
+        count = count + one(jnp.logical_and(settled, jnp.logical_or(mutual, peer < g)))
+
+        @pl.when(jnp.logical_and(settled, jnp.logical_or(mutual, peer > g)))
         def _():
             greet((peer, b))
+
+    @pl.when(source)
+    def _():
+        for other in range(4, 8):
+            greet((other, b))
 
     @pl.when(plain_in)
     def _():
@@ -237,7 +245,7 @@
 
     for i, peer in enumerate(peers):
 
-        @pl.when(jnp.logical_and(ordered, peer < g))
+        @pl.when(jnp.logical_and(jnp.logical_and(ordered, settled), peer < g))
         def _():
             tell(i, (peer, b))
 
@@ -281,7 +289,7 @@
         peer = g - place + target
         cs = copies(4 + 4 * i, quad.at[0], quad_assign.at[0], quad.at[i], quad_assign.at[i], (peer, b))
 
-        @pl.when(jnp.logical_and(ordered, peer > g))
+        @pl.when(jnp.logical_and(jnp.logical_and(ordered, settled), peer > g))
         def _():
             pl.semaphore_wait(ready.at[i], 1)
 
@@ -302,13 +310,12 @@
 
     samples[...] = jnp.zeros(samples.shape, f32)
     slot = lax.rem(round_, 4)
-    results = [pltpu.make_async_copy(lags.at[k], out.at[k], local.at[9 + k]) for k in range(2)]
 
     def other_row(station, comp):
         return 4 * comp + station
 
     def side(step, carry):
-        which = step + one(first) - 2 * step * one(first)
+        which = exclusive_or(step, one(jnp.logical_and(first, near_half)))
 
         @pl.when(which == 0)
         def _():
@@ -329,9 +336,7 @@
         for row in range(12):
             for comp in range(3):
                 at = 16 * row + 4 * comp
-                lags[which, row // 3, row % 3, comp] = result[at : at + 4, :LAGS].astype(bf16)
-        for k in range(2):
-            pl.when(which == k)(results[k].start)
+                out[which, row // 3, row % 3, comp] = result[at : at + 4, :LAGS].astype(bf16)
         return carry
 
     lax.fori_loop(0, 2, side, 0)
@@ -340,7 +345,13 @@
     for cs in to_quad[1:]:
         wait_send(cs)
     wait_send(to_near)
-    for c in results:
+
+
+def place_kernel(both, within, between, sems):
+    copies = [pltpu.make_async_copy(both.at[k], out, sems.at[k]) for k, out in enumerate((within, between))]
+    for c in copies:
+        c.start()
+    for c in copies:
         c.wait()
 
 
@@ -355,7 +366,7 @@
         correlate_kernel,
         out_shape=jax.ShapeDtypeStruct(result, bf16),
         in_specs=[hbm] * 7,
-        out_specs=anywhere,
+        out_specs=pl.BlockSpec(memory_space=pltpu.VMEM),
         scratch_shapes=[
             pltpu.VMEM(block, bf16),
             pltpu.VMEM((2,) + block, bf16),
@@ -370,7 +381,6 @@
             pltpu.VMEM((32, 1280), f32),
             *(pltpu.VMEM((32, NF), f32) for _ in range(4)),
             pltpu.VMEM((192, 2 * NF), bf16),
-            pltpu.VMEM(result, bf16),
             pltpu.SemaphoreType.DMA((20,)),
             pltpu.SemaphoreType.DMA((11,)),
             pltpu.SemaphoreType.REGULAR((5,)),
@@ -378,7 +388,16 @@
         compiler_params=pltpu.CompilerParams(collective_id=0, has_side_effects=True, vmem_limit_bytes=32 << 20),
         name="correlate",
     )(*(pltpu.with_memory_space_constraint(v, pltpu.HBM) for v in (traces, assign, matching, *tables_)))
-    return tuple(jnp.transpose(v, (0, 3, 1, 2, 4)) for v in (both[1], both[0]))
+    within, between = pl.pallas_call(
+        place_kernel,
+        out_shape=(jax.ShapeDtypeStruct(result[1:], bf16),) * 2,
+        in_specs=[anywhere],
+        out_specs=(anywhere, anywhere),
+        scratch_shapes=[pltpu.SemaphoreType.DMA((2,))],
+        compiler_params=pltpu.CompilerParams(vmem_limit_bytes=16 << 20),
+        name="place",
+    )(both)
+    return tuple(jnp.transpose(v, (0, 3, 1, 2, 4)) for v in (between, within))
 
 
 def solution(mesh):

time: 25.1 us -> 24.1 us (0.960)
  the two profiles are of different devices: /device:TPU:160 before, /device:TPU:38 now
where the time goes in v5:
time: 24.1 us; the launch traced here: 24 us
  Pallas kernels  23.3 us (97%)
  between operations  0.64 us (3%)
    pallas_call x1, Pallas kernels, shards(): pl.pallas_call(correlate_kernel, out_shape=jax.ShapeDtypeStruct(result, b...  22.6 us
    pallas_call x1, Pallas kernels, shards(): pl.pallas_call(place_kernel, out_shape=(jax.ShapeDtypeStruct(result[1:],...  0.73 us

profile of v5, /device:TPU:38, one launch (start us, length us, event | category | flops | bytes accessed | tf_op | source)
XLA Modules:
  0.0 24.0 jit_solution(6583875527011046404)
XLA Ops:
  0.6 22.6 %correlate.1.both = bf16[2,4,3,3,4,401]{5,4,3,2,1,0:T(4,128)(2,1)S(1)} custom-call(bf16[4,3,2,1200]{3,2,1,0:T(2,128)(2,1)} %traces.1, s32[1,4]{1,0:T(1,128)} %bitcast.3, s32[1,8]{1,0:T(1,128)} %matching_hbm.1, bf16[512,512]{1,0:T(8,128)(2,1)} %constant.8.clone.full_hbm, bf16[512,256]{1,0:T(8,128)(2,1)} %constant.9.clone.half_hbm, ...), custom_call_target="tpu_custom_call" | custom-call | tf_op jit(solution)/shard_map/correlate/pallas_call | solution.py:365
  23.2 0.7 %place.1 = (bf16[4,3,3,4,401]{4,3,2,1,0:T(4,128)(2,1)}, bf16[4,3,3,4,401]{4,3,2,1,0:T(4,128)(2,1)}) custom-call(bf16[2,4,3,3,4,401]{5,4,3,2,1,0:T(4,128)(2,1)S(1)} %correlate.1.both), custom_call_target="tpu_custom_call" | custom-call | tf_op jit(solution)/shard_map/place/pallas_call | solution.py:391

commit v6 on v5

--- a/solution.py
+++ b/solution.py
@@ -259,9 +259,24 @@
         def _():
             pl.semaphore_wait(ready.at[i], 1)
 
-    to_pair = copies(4, traces, assign, pair.at[1], pair_assign.at[1], (g4, b))
+    def halves(base, source, source_assign, target, target_assign, device):
+        parts = (
+            (source.at[pl.ds(0, 2)], target.at[pl.ds(0, 2)]),
+            (source_assign, target_assign),
+            (source.at[pl.ds(2, 2)], target.at[pl.ds(2, 2)]),
+        )
+        cs = [
+            pltpu.make_async_remote_copy(
+                a, t, sems.at[base + 2 * i], sems.at[base + 2 * i + 1], device_id=device, device_id_type=MESH
+            )
+            for i, (a, t) in enumerate(parts)
+        ]
+        return cs[:2], cs[2:]
+
+    to_pair = halves(4, traces, assign, pair.at[1], pair_assign.at[1], (g4, b))
     wait_ready(0)
-    start(to_pair)
+    start(to_pair[0])
+    start(to_pair[1])
 
     def step_up():
         pl.semaphore_wait(ready.at[4], 1)
@@ -274,35 +289,61 @@
     order = inverse_order(lambda r: own_assign[0, r])
     load_samples(samples, lambda r, comp: own[r, comp], order, lambda station, comp: 3 * station + comp)
     transform(samples, full, half, twiddle, left_re, left_im)
-    wait_recv(to_pair)
-
     round_ = matching[0, 0]
     bit = lax.rem(lax.div(round_, 4), 2)
-    quad[0] = pair[bit]
-    for r in range(4):
-        quad_assign[0, 0, r] = pair_assign[bit, 0, r]
     place = lax.rem(g, 4)
     to_quad = []
     for k in range(3):
         target = k + one(place <= k)
         i = exclusive_or(place, target)
         peer = g - place + target
-        cs = copies(4 + 4 * i, quad.at[0], quad_assign.at[0], quad.at[i], quad_assign.at[i], (peer, b))
+        cs = halves(4 + 6 * i, quad.at[0], quad_assign.at[0], quad.at[i], quad_assign.at[i], (peer, b))
+        to_quad.append((i, peer, cs))
+
+    def when_ready(k):
+        i, peer, _ = to_quad[k]
 
         @pl.when(jnp.logical_and(jnp.logical_and(ordered, settled), peer > g))
         def _():
             pl.semaphore_wait(ready.at[i], 1)
 
-        start(cs)
-        to_quad.append(cs)
-        if k == 0:
-
-            @pl.when(below)
-            def _():
-                wait_send(cs)
+    def keep(h):
+        rows = pl.ds(2 * h, 2)
+        quad[0, rows] = jnp.where(bit == 1, pair[1, rows], pair[0, rows])
+
+    wait_recv(to_pair[0])
+    for r in range(4):
+        quad_assign[0, 0, r] = jnp.where(bit == 1, pair_assign[1, 0, r], pair_assign[0, 0, r])
+    keep(0)
+    when_ready(0)
+    start(to_quad[0][2][0])
+
+    @pl.when(above)
+    def _():
+        for k in (1, 2):
+            when_ready(k)
+            start(to_quad[k][2][0])
+
+    wait_recv(to_pair[1])
+    keep(1)
+    start(to_quad[0][2][1])
+
+    @pl.when(below)
+    def _():
+        wait_send(to_quad[0][2][0])
+        for k in (1, 2):
+            when_ready(k)
+            start(to_quad[k][2][0])
+            start(to_quad[k][2][1])
+        wait_send(to_quad[0][2][1])
+
+    @pl.when(above)
+    def _():
+        for k in (1, 2):
+            start(to_quad[k][2][1])
 
     from_quad = [
-        copies(4 + 4 * i, quad.at[0], quad_assign.at[0], quad.at[i], quad_assign.at[i], (peers[i], b))
+        halves(4 + 6 * i, quad.at[0], quad_assign.at[0], quad.at[i], quad_assign.at[i], (peers[i], b))
         for i in range(1, 4)
     ]
 
@@ -315,7 +356,8 @@
         return 4 * comp + station
 
     def side(step, carry):
-        which = exclusive_or(step, one(jnp.logical_and(first, near_half)))
+        late = one(b < 16)
+        which = exclusive_or(step, one(jnp.logical_and(jnp.logical_and(first, near_half), jnp.logical_or(above, g <= late))))
 
         @pl.when(which == 0)
         def _():
@@ -326,7 +368,8 @@
         @pl.when(which == 1)
         def _():
             for cs in from_quad:
-                wait_recv(cs)
+                wait_recv(cs[0])
+                wait_recv(cs[1])
             order = inverse_order(lambda r: quad_assign[slot, 0, r])
             load_samples(samples, lambda r, comp: quad[slot, r, comp], order, other_row)
 
@@ -340,10 +383,17 @@
         return carry
 
     lax.fori_loop(0, 2, side, 0)
-    wait_send(to_pair)
-    pl.when(above)(lambda: wait_send(to_quad[0]))
-    for cs in to_quad[1:]:
-        wait_send(cs)
+    wait_send(to_pair[0])
+    wait_send(to_pair[1])
+
+    @pl.when(above)
+    def _():
+        wait_send(to_quad[0][2][0])
+        wait_send(to_quad[0][2][1])
+
+    for _i, _peer, cs in to_quad[1:]:
+        wait_send(cs[0])
+        wait_send(cs[1])
     wait_send(to_near)
 
 
@@ -381,7 +431,7 @@
             pltpu.VMEM((32, 1280), f32),
             *(pltpu.VMEM((32, NF), f32) for _ in range(4)),
             pltpu.VMEM((192, 2 * NF), bf16),
-            pltpu.SemaphoreType.DMA((20,)),
+            pltpu.SemaphoreType.DMA((28,)),
             pltpu.SemaphoreType.DMA((11,)),
             pltpu.SemaphoreType.REGULAR((5,)),
         ],

time: 24.1 us -> 23.2 us (0.963)
  the two profiles are of different devices: /device:TPU:38 before, /device:TPU:128 now
where the time goes in v6:
time: 23.2 us; the launch traced here: 23.1 us
  Pallas kernels  22.5 us (97%)
  between operations  0.64 us (3%)
    pallas_call x1, Pallas kernels, shards(): pl.pallas_call(correlate_kernel, out_shape=jax.ShapeDtypeStruct(result, b...  21.7 us
    pallas_call x1, Pallas kernels, shards(): pl.pallas_call(place_kernel, out_shape=(jax.ShapeDtypeStruct(result[1:],...  0.73 us

profile of v6, /device:TPU:128, one launch (start us, length us, event | category | flops | bytes accessed | tf_op | source)
XLA Modules:
  0.0 23.1 jit_solution(4636160513467459077)
XLA Ops:
  0.6 21.7 %correlate.1.both = bf16[2,4,3,3,4,401]{5,4,3,2,1,0:T(4,128)(2,1)S(1)} custom-call(bf16[4,3,2,1200]{3,2,1,0:T(2,128)(2,1)} %traces.1, s32[1,4]{1,0:T(1,128)} %bitcast.3, s32[1,8]{1,0:T(1,128)} %matching_hbm.1, bf16[512,512]{1,0:T(8,128)(2,1)} %constant.8.clone.full_hbm, bf16[512,256]{1,0:T(8,128)(2,1)} %constant.9.clone.half_hbm, ...), custom_call_target="tpu_custom_call" | custom-call | tf_op jit(solution)/shard_map/correlate/pallas_call | solution.py:415
  22.4 0.7 %place.1 = (bf16[4,3,3,4,401]{4,3,2,1,0:T(4,128)(2,1)}, bf16[4,3,3,4,401]{4,3,2,1,0:T(4,128)(2,1)}) custom-call(bf16[2,4,3,3,4,401]{5,4,3,2,1,0:T(4,128)(2,1)S(1)} %correlate.1.both), custom_call_target="tpu_custom_call" | custom-call | tf_op jit(solution)/shard_map/place/pallas_call | solution.py:441

commit v7 on v6

--- a/solution.py
+++ b/solution.py
@@ -61,13 +61,15 @@
     return order
 
 
-def load_samples(samples, block, order, row):
+def load_samples(samples, block, order, row, twice=False):
     for station in range(4):
         for comp in range(3):
             both = block(order[station], comp).astype(f32)
             for w in range(2):
                 at = 16 * w + row(station, comp)
                 samples[at : at + 1, 0:NSAMP] = both[w : w + 1]
+                if twice and comp == 2:
+                    samples[at + 4 : at + 5, 0:NSAMP] = both[w : w + 1]
 
 
 def transform(samples, full, half, twiddle, real, imag):
@@ -104,21 +106,31 @@
 
 
 def multiply(left, right, cross):
+    upper = lax.broadcasted_iota(jnp.int32, (8, 256), 0) < 4
     for q in range(3):
         lanes = slice(256 * q, 256 * q + 256)
-        other = [[part[16 * w : 16 * w + 16, lanes] for part in right] for w in range(2)]
-        for row in range(12):
+
+        def product(rows, at):
             re = im = None
             for w in range(2):
-                at = 16 * w + row
-                left_re = jnp.broadcast_to(left[0][at : at + 1, lanes], (16, 256))
-                left_im = jnp.broadcast_to(left[1][at : at + 1, lanes], (16, 256))
-                right_re, right_im = other[w]
-                a = left_re * right_re + left_im * right_im
-                d = left_re * right_im - left_im * right_re
+                left_re, left_im = (
+                    [jnp.broadcast_to(part[16 * w + row : 16 * w + row + 1, lanes], (8, 256)) for row in rows]
+                    for part in left
+                )
+                if len(rows) == 2:
+                    left_re, left_im = [jnp.where(upper, *left_re)], [jnp.where(upper, *left_im)]
+                right_re, right_im = (part[16 * w + at : 16 * w + at + 8, lanes] for part in right)
+                a = left_re[0] * right_re + left_im[0] * right_im
+                d = left_re[0] * right_im - left_im[0] * right_re
                 re, im = (a, d) if re is None else (re + a, im + d)
-            cross[16 * row : 16 * row + 16, lanes] = re.astype(bf16)
-            cross[16 * row : 16 * row + 16, NF + 256 * q : NF + 256 * q + 256] = im.astype(bf16)
+            return re, im
+
+        for four in range(3):
+            row = 4 * four
+            parts = [product((row + k,), 0) for k in range(4)] + [product((row + k, row + k + 1), 8) for k in (0, 2)]
+            rows = slice(48 * four, 48 * four + 48)
+            for k, column in enumerate((256 * q, NF + 256 * q)):
+                cross[rows, column : column + 256] = jnp.concatenate([p[k] for p in parts], axis=0).astype(bf16)
 
 
 def exclusive_or(a, b):
@@ -363,7 +375,7 @@
         def _():
             wait_recv(to_near)
             order = inverse_order(lambda r: near_assign[0, r])
-            load_samples(samples, lambda r, comp: near[r, comp], order, other_row)
+            load_samples(samples, lambda r, comp: near[r, comp], order, other_row, True)
 
         @pl.when(which == 1)
         def _():
@@ -371,14 +383,14 @@
                 wait_recv(cs[0])
                 wait_recv(cs[1])
             order = inverse_order(lambda r: quad_assign[slot, 0, r])
-            load_samples(samples, lambda r, comp: quad[slot, r, comp], order, other_row)
+            load_samples(samples, lambda r, comp: quad[slot, r, comp], order, other_row, True)
 
         transform(samples, full, half, twiddle, right_re, right_im)
         multiply((left_re, left_im), (right_re, right_im), cross)
         result = jnp.dot(cross[...], inverse[...], preferred_element_type=f32) * SCALE
         for row in range(12):
             for comp in range(3):
-                at = 16 * row + 4 * comp
+                at = 48 * (row // 4) + (32 + 4 * (row % 4) if comp == 2 else 8 * (row % 4) + 4 * comp)
                 out[which, row // 3, row % 3, comp] = result[at : at + 4, :LAGS].astype(bf16)
         return carry
 
@@ -430,7 +442,7 @@
             *(pltpu.VMEM(t.shape, t.dtype) for t in tables_),
             pltpu.VMEM((32, 1280), f32),
             *(pltpu.VMEM((32, NF), f32) for _ in range(4)),
-            pltpu.VMEM((192, 2 * NF), bf16),
+            pltpu.VMEM((144, 2 * NF), bf16),
             pltpu.SemaphoreType.DMA((28,)),
             pltpu.SemaphoreType.DMA((11,)),
             pltpu.SemaphoreType.REGULAR((5,)),

time: 23.2 us -> 23.2 us (level)
  no operation moved by 1% of the time
where the time goes in v7:
time: 23.2 us; the launch traced here: 23.1 us
  Pallas kernels  22.4 us (97%)
  between operations  0.64 us (3%)
    pallas_call x1, Pallas kernels, shards(): pl.pallas_call(correlate_kernel, out_shape=jax.ShapeDtypeStruct(result, b...  21.7 us
    pallas_call x1, Pallas kernels, shards(): pl.pallas_call(place_kernel, out_shape=(jax.ShapeDtypeStruct(result[1:],...  0.73 us

profile of v7, /device:TPU:128, one launch (start us, length us, event | category | flops | bytes accessed | tf_op | source)
XLA Modules:
  0.0 23.1 jit_solution(12561976659928226033)
XLA Ops:
  0.6 21.7 %correlate.1.both = bf16[2,4,3,3,4,401]{5,4,3,2,1,0:T(4,128)(2,1)S(1)} custom-call(bf16[4,3,2,1200]{3,2,1,0:T(2,128)(2,1)} %traces.1, s32[1,4]{1,0:T(1,128)} %bitcast.3, s32[1,8]{1,0:T(1,128)} %matching_hbm.1, bf16[512,512]{1,0:T(8,128)(2,1)} %constant.8.clone.full_hbm, bf16[512,256]{1,0:T(8,128)(2,1)} %constant.9.clone.half_hbm, ...), custom_call_target="tpu_custom_call" | custom-call | tf_op jit(solution)/shard_map/correlate/pallas_call | solution.py:427
  22.4 0.7 %place.1 = (bf16[4,3,3,4,401]{4,3,2,1,0:T(4,128)(2,1)}, bf16[4,3,3,4,401]{4,3,2,1,0:T(4,128)(2,1)}) custom-call(bf16[2,4,3,3,4,401]{5,4,3,2,1,0:T(4,128)(2,1)S(1)} %correlate.1.both), custom_call_target="tpu_custom_call" | custom-call | tf_op jit(solution)/shard_map/place/pallas_call | solution.py:453

commit v8 on v7

--- a/solution.py
+++ b/solution.py
@@ -17,6 +17,9 @@
 HALF = 200
 LAGS = 401
 FAST = 256
+PIECES = 4
+HEAD = 4
+STEP = 2 * PIECES + 2
 EPSILON = 1e-05
 SCALE = 2.0 / (PLEN * math.sqrt(NSAMP * WIN))
 ROOT3 = math.sqrt(3) / 2
@@ -271,24 +274,21 @@
         def _():
             pl.semaphore_wait(ready.at[i], 1)
 
-    def halves(base, source, source_assign, target, target_assign, device):
-        parts = (
-            (source.at[pl.ds(0, 2)], target.at[pl.ds(0, 2)]),
-            (source_assign, target_assign),
-            (source.at[pl.ds(2, 2)], target.at[pl.ds(2, 2)]),
-        )
+    def pieces(base, source, source_assign, target, target_assign, device):
+        rows = source.shape[0] // PIECES
+        parts = [(source.at[pl.ds(rows * h, rows)], target.at[pl.ds(rows * h, rows)]) for h in range(PIECES)]
         cs = [
             pltpu.make_async_remote_copy(
                 a, t, sems.at[base + 2 * i], sems.at[base + 2 * i + 1], device_id=device, device_id_type=MESH
             )
-            for i, (a, t) in enumerate(parts)
+            for i, (a, t) in enumerate([*parts, (source_assign, target_assign)])
         ]
-        return cs[:2], cs[2:]
-
-    to_pair = halves(4, traces, assign, pair.at[1], pair_assign.at[1], (g4, b))
+        return [[cs[0], cs[-1]]] + [[c] for c in cs[1:-1]]
+
+    to_pair = pieces(4, traces, assign, pair.at[1], pair_assign.at[1], (g4, b))
     wait_ready(0)
-    start(to_pair[0])
-    start(to_pair[1])
+    for cs in to_pair:
+        start(cs)
 
     def step_up():
         pl.semaphore_wait(ready.at[4], 1)
@@ -309,7 +309,7 @@
         target = k + one(place <= k)
         i = exclusive_or(place, target)
         peer = g - place + target
-        cs = halves(4 + 6 * i, quad.at[0], quad_assign.at[0], quad.at[i], quad_assign.at[i], (peer, b))
+        cs = pieces(4 + STEP * i, quad.at[0], quad_assign.at[0], quad.at[i], quad_assign.at[i], (peer, b))
         to_quad.append((i, peer, cs))
 
     def when_ready(k):
@@ -320,42 +320,38 @@
             pl.semaphore_wait(ready.at[i], 1)
 
     def keep(h):
-        rows = pl.ds(2 * h, 2)
+        rows = pl.ds(h * (4 // PIECES), 4 // PIECES)
         quad[0, rows] = jnp.where(bit == 1, pair[1, rows], pair[0, rows])
 
-    wait_recv(to_pair[0])
-    for r in range(4):
-        quad_assign[0, 0, r] = jnp.where(bit == 1, pair_assign[1, 0, r], pair_assign[0, 0, r])
-    keep(0)
-    when_ready(0)
-    start(to_quad[0][2][0])
-
-    @pl.when(above)
-    def _():
+    for h in range(PIECES):
+        wait_recv(to_pair[h])
+        if h == 0:
+            for r in range(4):
+                quad_assign[0, 0, r] = jnp.where(bit == 1, pair_assign[1, 0, r], pair_assign[0, 0, r])
+            when_ready(0)
+        keep(h)
+        start(to_quad[0][2][h])
+
+        @pl.when(above)
+        def _():
+            for k in (1, 2):
+                if h == 0:
+                    when_ready(k)
+                start(to_quad[k][2][h])
+
+    @pl.when(below)
+    def _():
+        for h in range(PIECES // HEAD):
+            wait_send(to_quad[0][2][h])
         for k in (1, 2):
             when_ready(k)
-            start(to_quad[k][2][0])
-
-    wait_recv(to_pair[1])
-    keep(1)
-    start(to_quad[0][2][1])
-
-    @pl.when(below)
-    def _():
-        wait_send(to_quad[0][2][0])
-        for k in (1, 2):
-            when_ready(k)
-            start(to_quad[k][2][0])
-            start(to_quad[k][2][1])
-        wait_send(to_quad[0][2][1])
-
-    @pl.when(above)
-    def _():
-        for k in (1, 2):
-            start(to_quad[k][2][1])
+            for cs in to_quad[k][2]:
+                start(cs)
+        for h in range(PIECES // HEAD, PIECES):
+            wait_send(to_quad[0][2][h])
 
     from_quad = [
-        halves(4 + 6 * i, quad.at[0], quad_assign.at[0], quad.at[i], quad_assign.at[i], (peers[i], b))
+        pieces(4 + STEP * i, quad.at[0], quad_assign.at[0], quad.at[i], quad_assign.at[i], (peers[i], b))
         for i in range(1, 4)
     ]
 
@@ -380,8 +376,8 @@
         @pl.when(which == 1)
         def _():
             for cs in from_quad:
-                wait_recv(cs[0])
-                wait_recv(cs[1])
+                for piece in cs:
+                    wait_recv(piece)
             order = inverse_order(lambda r: quad_assign[slot, 0, r])
             load_samples(samples, lambda r, comp: quad[slot, r, comp], order, other_row, True)
 
@@ -395,17 +391,17 @@
         return carry
 
     lax.fori_loop(0, 2, side, 0)
-    wait_send(to_pair[0])
-    wait_send(to_pair[1])
+    for cs in to_pair:
+        wait_send(cs)
 
     @pl.when(above)
     def _():
-        wait_send(to_quad[0][2][0])
-        wait_send(to_quad[0][2][1])
-
-    for _i, _peer, cs in to_quad[1:]:
-        wait_send(cs[0])
-        wait_send(cs[1])
+        for cs in to_quad[0][2]:
+            wait_send(cs)
+
+    for _i, _peer, sent in to_quad[1:]:
+        for cs in sent:
+            wait_send(cs)
     wait_send(to_near)
 
 
@@ -443,7 +439,7 @@
             pltpu.VMEM((32, 1280), f32),
             *(pltpu.VMEM((32, NF), f32) for _ in range(4)),
             pltpu.VMEM((144, 2 * NF), bf16),
-            pltpu.SemaphoreType.DMA((28,)),
+            pltpu.SemaphoreType.DMA((4 + 4 * STEP,)),
             pltpu.SemaphoreType.DMA((11,)),
             pltpu.SemaphoreType.REGULAR((5,)),
         ],

time: 23.2 us -> 23.2 us (level)
  no operation moved by 1% of the time
where the time goes in v8:
time: 23.2 us; the launch traced here: 23.1 us
  Pallas kernels  22.5 us (97%)
  between operations  0.64 us (3%)
    pallas_call x1, Pallas kernels, shards(): pl.pallas_call(correlate_kernel, out_shape=jax.ShapeDtypeStruct(result, b...  21.7 us
    pallas_call x1, Pallas kernels, shards(): pl.pallas_call(place_kernel, out_shape=(jax.ShapeDtypeStruct(result[1:],...  0.73 us

profile of v8, /device:TPU:128, one launch (start us, length us, event | category | flops | bytes accessed | tf_op | source)
XLA Modules:
  0.0 23.1 jit_solution(14012211438541051278)
XLA Ops:
  0.6 21.7 %correlate.1.both = bf16[2,4,3,3,4,401]{5,4,3,2,1,0:T(4,128)(2,1)S(1)} custom-call(bf16[4,3,2,1200]{3,2,1,0:T(2,128)(2,1)} %traces.1, s32[1,4]{1,0:T(1,128)} %bitcast.3, s32[1,8]{1,0:T(1,128)} %matching_hbm.1, bf16[512,512]{1,0:T(8,128)(2,1)} %constant.8.clone.full_hbm, bf16[512,256]{1,0:T(8,128)(2,1)} %constant.9.clone.half_hbm, ...), custom_call_target="tpu_custom_call" | custom-call | tf_op jit(solution)/shard_map/correlate/pallas_call | solution.py:423
  22.4 0.7 %place.1 = (bf16[4,3,3,4,401]{4,3,2,1,0:T(4,128)(2,1)}, bf16[4,3,3,4,401]{4,3,2,1,0:T(4,128)(2,1)}) custom-call(bf16[2,4,3,3,4,401]{5,4,3,2,1,0:T(4,128)(2,1)S(1)} %correlate.1.both), custom_call_target="tpu_custom_call" | custom-call | tf_op jit(solution)/shard_map/place/pallas_call | solution.py:449

commit v9 on v8

--- a/solution.py
+++ b/solution.py
@@ -254,10 +254,6 @@
 
     to_near = copies(0, traces, assign, near, near_assign, (g, right))
 
-    @pl.when(plain_out)
-    def _():
-        start(to_near)
-
     for i, peer in enumerate(peers):
 
         @pl.when(jnp.logical_and(jnp.logical_and(ordered, settled), peer < g))
@@ -268,6 +264,10 @@
     def _():
         tell(4, (g, left))
         tell(4, (opposite, left))
+
+    @pl.when(plain_out)
+    def _():
+        start(to_near)
 
     def wait_ready(i):
         @pl.when(jnp.logical_and(ordered, peers[i] > g))

time: 23.2 us -> 23.3 us (level)
  no operation moved by 1% of the time
where the time goes in v9:
time: 23.3 us; the launch traced here: 23.1 us
  Pallas kernels  22.5 us (97%)
  between operations  0.64 us (3%)
    pallas_call x1, Pallas kernels, shards(): pl.pallas_call(correlate_kernel, out_shape=jax.ShapeDtypeStruct(result, b...  21.8 us
    pallas_call x1, Pallas kernels, shards(): pl.pallas_call(place_kernel, out_shape=(jax.ShapeDtypeStruct(result[1:],...  0.73 us

profile of v9, /device:TPU:128, one launch (start us, length us, event | category | flops | bytes accessed | tf_op | source)
XLA Modules:
  0.0 23.1 jit_solution(13660635843047966026)
XLA Ops:
  0.6 21.8 %correlate.1.both = bf16[2,4,3,3,4,401]{5,4,3,2,1,0:T(4,128)(2,1)S(1)} custom-call(bf16[4,3,2,1200]{3,2,1,0:T(2,128)(2,1)} %traces.1, s32[1,4]{1,0:T(1,128)} %bitcast.3, s32[1,8]{1,0:T(1,128)} %matching_hbm.1, bf16[512,512]{1,0:T(8,128)(2,1)} %constant.8.clone.full_hbm, bf16[512,256]{1,0:T(8,128)(2,1)} %constant.9.clone.half_hbm, ...), custom_call_target="tpu_custom_call" | custom-call | tf_op jit(solution)/shard_map/correlate/pallas_call | solution.py:423
  22.4 0.7 %place.1 = (bf16[4,3,3,4,401]{4,3,2,1,0:T(4,128)(2,1)}, bf16[4,3,3,4,401]{4,3,2,1,0:T(4,128)(2,1)}) custom-call(bf16[2,4,3,3,4,401]{5,4,3,2,1,0:T(4,128)(2,1)S(1)} %correlate.1.both), custom_call_target="tpu_custom_call" | custom-call | tf_op jit(solution)/shard_map/place/pallas_call | solution.py:449
